TPU v7x, 32 devices: a whole 2x2x4 slice. The times are simulated.
32 devices in a mesh: groups: 2 (over y), wide: 8 (over z, x), narrow: 2 (over core).
Axes of the slice: x: 2, y: 2, z: 4, core: 2. Of those that a mesh axis runs over, the one named last changes fastest.
Arguments:
- queries: bfloat16 [4, 2048, 64], P(('groups', 'narrow'), 'wide'), parts along dimension 0, may hold values from -6 to 6
- key_rows: bfloat16 [4, 2048, 64], P(('groups', 'narrow'), 'wide'), parts along dimension 0, may hold values from -6 to 6
- values: bfloat16 [4, 2048, 64], P(('groups', 'narrow'), 'wide'), parts along dimension 0, may hold values from -6 to 6
- log_gate: float32 [4, 2048], P(('groups', 'narrow'), 'wide'), parts along dimension 0, may hold values from -0.8 to 0, as said below
- lengths: int32 [4], P(('groups', 'narrow')), parts along dimension 0, may hold values from 1024 to 2048
- cont_queries: bfloat16 [160, 64], P(('groups', 'wide', 'narrow')), parts along dimension 0, may hold values from -6 to 6
- cont_prompt: int32 [160], P(('groups', 'wide', 'narrow')), parts along dimension 0, may hold values from 0 to 1
Outputs:
- prompt_out: bfloat16 [4, 2048, 64], P(('groups', 'narrow'), 'wide'), parts along dimension 0
- cont_out: bfloat16 [160, 64], P(('groups', 'wide', 'narrow')), parts along dimension 0
There are 2 independent parts, one for each index of `groups`. A program takes and returns all parts, laid end to end along the dimension named above; each array names one. Nothing has to cross between parts.
Inputs may be any that keep to these rules, and one draw needn't show every extreme that they name: `log_gate`: gates only shrink the state: every entry is at most zero.
All inputs are finite; a program needn't handle non-finite values.
Results may differ from a plain program's by a relative error of at most 0.0067.
Values may be sent and summed in bfloat16 or wider, within the bound.
A program may use at most 64 MiB of HBM per device.

v0:
```python
import jax
import jax.numpy as jnp
import numpy as np
from jax import lax
from jax.sharding import PartitionSpec as P

epsilon = 1e-06
block_rows = 1024


def rms_rows(running):
    return running * lax.rsqrt(jnp.mean(running * running, axis=-1, keepdims=True) + epsilon)


def extend_zeros(table, pad_count):
    return np.concatenate([table, np.zeros((pad_count,), table.dtype)])


def pair_tables(head_width, shard_count):
    lead_index, trail_index = np.triu_indices(head_width)
    doubled = np.where(lead_index == trail_index, 1.0, 2.0)
    feature_count = lead_index.shape[0]
    padded_rows = -(-feature_count // shard_count) * shard_count
    block_width = min(block_rows, padded_rows)
    full_length = -(-padded_rows // block_width) * block_width
    pad_count = full_length - lead_index.shape[0]
    lead_index = extend_zeros(lead_index, pad_count).astype(np.int32)
    trail_index = extend_zeros(trail_index, pad_count).astype(np.int32)
    doubled = extend_zeros(doubled, pad_count).astype(np.float32)
    live_pairs = (doubled > 0).astype(np.float32)
    return (
        jnp.asarray(lead_index),
        jnp.asarray(trail_index),
        jnp.asarray(doubled),
        jnp.asarray(live_pairs),
        padded_rows,
        block_width,
        full_length,
    )


def pair_block(rows, lead_part, trail_part, forget_multiplier):
    leading_columns = jnp.take(rows, lead_part, axis=1).astype(jnp.float32)
    right_cols = jnp.take(rows, trail_part, axis=1).astype(jnp.float32)
    return (leading_columns * right_cols * forget_multiplier[None, :]).astype(jnp.bfloat16)


def block_state(key_rows, spread, tables):
    lead_all, trail_all, doubled_all, live_pairs, padded_rows, block_width, full_length = tables
    head_width = key_rows.shape[1]

    def fill_block(block_index, state):
        first_row = block_index * block_width
        features = pair_block(
            key_rows,
            lax.dynamic_slice_in_dim(lead_all, first_row, block_width),
            lax.dynamic_slice_in_dim(trail_all, first_row, block_width),
            lax.dynamic_slice_in_dim(live_pairs, first_row, block_width),
        )
        state_block = lax.dot_general(
            features, spread, (((0,), (0,)), ((), ())), preferred_element_type=jnp.float32
        )
        return lax.dynamic_update_slice_in_dim(
            state, state_block.astype(jnp.bfloat16), first_row, 0
        )

    initial = jnp.zeros((full_length, head_width), jnp.bfloat16)
    return lax.fori_loop(0, full_length // block_width, fill_block, initial)[:padded_rows]


def carried_read(query_rows, carried, tables):
    lead_all, trail_all, doubled_all, live_pairs, padded_rows, block_width, full_length = tables
    row_count, head_width = query_rows.shape
    if full_length > padded_rows:
        carried = jnp.pad(carried, ((0, full_length - padded_rows), (0, 0)))

    def add_block(block_index, running):
        first_row = block_index * block_width
        features = pair_block(
            query_rows,
            lax.dynamic_slice_in_dim(lead_all, first_row, block_width),
            lax.dynamic_slice_in_dim(trail_all, first_row, block_width),
            lax.dynamic_slice_in_dim(doubled_all, first_row, block_width),
        )
        state_rows = lax.dynamic_slice_in_dim(carried, first_row, block_width, 0)
        return running + jnp.dot(features, state_rows, preferred_element_type=jnp.float32)

    return lax.fori_loop(
        0, full_length // block_width, add_block, jnp.zeros((row_count, head_width), jnp.float32)
    )


def owner_prefix(sent_slices, totals):
    shard_count = totals.shape[0]
    inclusive = jnp.cumsum(totals)
    exclusive = jnp.concatenate([jnp.zeros((1,), jnp.float32), inclusive])
    target = lax.iota(jnp.int32, shard_count + 1)[:, None]
    source = lax.iota(jnp.int32, shard_count)[None, :]
    weight = jnp.exp(jnp.where(source < target, exclusive[:, None] - inclusive[None, :], -jnp.inf))
    return jnp.einsum(
        "wu,urn->wrn", weight, sent_slices.astype(jnp.float32), precision=lax.Precision.HIGHEST
    )


def prompt_rows(query_rows, key_rows, payload_lines, cumulative, live_mask, carried, tables):
    row_count, head_width = query_rows.shape
    scores = lax.dot_general(
        query_rows, key_rows, (((1,), (1,)), ((), ())), preferred_element_type=jnp.float32
    )
    row_ids = lax.iota(jnp.int32, row_count)
    lower_mask = row_ids[:, None] >= row_ids[None, :]
    decay_matrix = jnp.exp(
        jnp.where(lower_mask, cumulative[:, None] - cumulative[None, :], -jnp.inf)
    )
    weights = (scores * scores * decay_matrix * live_mask[None, :]).astype(jnp.bfloat16)
    local_term = jnp.dot(weights, payload_lines, preferred_element_type=jnp.float32)
    carried_term = carried_read(query_rows, carried, tables)
    running = local_term + jnp.exp(cumulative)[:, None] * carried_term
    return (live_mask[:, None] * rms_rows(running)).astype(jnp.bfloat16)


def on_device(queries, key_rows, values, log_gate, lengths, cont_queries, cont_prompt):
    wide_count = lax.axis_size("wide")
    lane_count = lax.axis_size("narrow")
    owner_index = lax.axis_index("wide")
    prompt_lane = lax.axis_index("narrow")
    query_rows = queries[0]
    own_keys = key_rows[0]
    payload_lines = values[0]
    row_count, head_width = own_keys.shape
    tables = pair_tables(head_width, wide_count)
    lead_all, trail_all, doubled_all = (tables[0], tables[1], tables[2])
    padded_rows = tables[4]
    rows_per = padded_rows // wide_count
    position = owner_index * row_count + lax.iota(jnp.int32, row_count)
    live_mask = (position < lengths[0]).astype(jnp.float32)
    cumulative = jnp.cumsum(log_gate[0] * live_mask)
    piece_number = cumulative[-1]
    scaled = live_mask * jnp.exp(piece_number - cumulative)
    spread = (scaled[:, None] * payload_lines.astype(jnp.float32)).astype(jnp.bfloat16)
    span_state = block_state(own_keys, spread, tables)
    totals = lax.all_gather(piece_number[None], "wide", axis=0, tiled=True)
    sent_slices = lax.all_to_all(
        span_state.reshape(wide_count, rows_per, head_width),
        "wide",
        split_axis=0,
        concat_axis=0,
        tiled=True,
    )
    rounded = owner_prefix(sent_slices, totals).astype(jnp.bfloat16)
    carried_slices = lax.all_to_all(
        rounded[:wide_count], "wide", split_axis=0, concat_axis=0, tiled=True
    )
    carried = carried_slices.reshape(padded_rows, head_width)
    final_slice = rounded[wide_count]
    prompt_out = prompt_rows(
        query_rows, own_keys, payload_lines, cumulative, live_mask, carried, tables
    )
    prompt_ids = lax.iota(jnp.int32, lane_count)[:, None]
    chosen = (cont_prompt[None, :] == prompt_ids)[:, :, None]
    masked = jnp.where(chosen, cont_queries[None, :, :], jnp.zeros_like(cont_queries)[None, :, :])
    pair_rows = lax.all_gather(masked, "narrow", axis=1, tiled=True)
    own_rows = lax.dynamic_index_in_dim(pair_rows, prompt_lane, 0, keepdims=False)
    initial = jnp.zeros((own_rows.shape[0], head_width), jnp.float32)
    shard_portion = lax.all_gather(final_slice, "wide", axis=0, tiled=True)
    piece_rows = shard_portion.shape[0]
    features = pair_block(
        own_rows,
        lax.slice_in_dim(lead_all, 0, piece_rows, axis=0),
        lax.slice_in_dim(trail_all, 0, piece_rows, axis=0),
        lax.slice_in_dim(doubled_all, 0, piece_rows, axis=0),
    )
    partial_value = initial + jnp.dot(features, shard_portion, preferred_element_type=jnp.float32)
    running = lax.psum_scatter(partial_value, "narrow", scatter_dimension=0, tiled=True)
    cont_out = rms_rows(running).astype(jnp.bfloat16)
    return (prompt_out[None], cont_out)


def solution(mesh):
    in_specs = (
        P(("groups", "narrow"), "wide", None),
        P(("groups", "narrow"), "wide", None),
        P(("groups", "narrow"), "wide", None),
        P(("groups", "narrow"), "wide"),
        P(("groups", "narrow")),
        P(("groups", "wide", "narrow"), None),
        P(("groups", "wide", "narrow")),
    )
    out_specs = (P(("groups", "narrow"), "wide", None), P(("groups", "wide", "narrow"), None))
    return jax.shard_map(
        on_device, mesh=mesh, in_specs=in_specs, out_specs=out_specs, check_vma=False
    )
```

profile of v0, /device:TPU:0, one launch (start us, length us, event | category | flops | bytes accessed | tf_op | source)
XLA Modules:
  0.0 162.9 jit_solution(10118833108402280067)
XLA Ops:
  1.3 0.7 compare_select_fusion.4
  2.0 0.3 reduce-window.19
  2.4 0.1 slice_reduce_fusion
  2.6 0.9 copy.25
  3.5 1.2 dynamic-slice
  4.7 1.3 slice_dynamic-update-slice_fusion
  6.0 0.6 exponential_select_fusion
  6.8 33.6 %while.29 = (s32[]{:T(128)}, bf16[3072,64]{0,1:T(8,128)(2,1)S(1)}, bf16[256,64]{0,1:T(8,128)(2,1)}, bf16[256,64]{1,0:T(8,128)(2,1)S(1)}, s32[]{:T(128)}, /*index...) while((s32[]{:T(128)}, bf16[3072,64]{0,1:T(8,128)(2,1)S(1)}, ...), condition=%wide.region_4.6_spmd.clone, body=%wide.region_3.5_spmd.sunk.clone.sunk | while | flops 35475460 | bytes 3522759 | solution.py:68
  6.8 0.7 fusion.85
  7.5 3.9 %gather_fusion = bf16[1024,256]{1,0:T(8,128)(2,1)S(1)} fusion(bf16[256,64]{0,1:T(8,128)(2,1)S(1)} %copy-done.1, s32[1024]{0:T(1024)S(1)} %get-tuple-element.395), kind=kCustom, calls=%fused_computation.2.clone.clone.1 | custom fusion | bytes 1052672 | tf_op jit(solution)/shard_map/while/body/eval_jaxpr/jit(_take)/gather | solution.py:44
  11.5 3.9 %gather_fusion.1 = bf16[1024,256]{1,0:T(8,128)(2,1)S(1)} fusion(bf16[256,64]{0,1:T(8,128)(2,1)S(1)} %copy-done.1, s32[1024]{0:T(1024)S(1)} %get-tuple-element.396), kind=kCustom, calls=%fused_computation.clone.clone.1 | custom fusion | bytes 1052672 | tf_op jit(solution)/shard_map/while/body/eval_jaxpr/jit(_take)/gather | solution.py:43
  15.4 0.7 fusion.86
  16.2 0.7 dynamic_slice.128
  16.8 1.1 fusion.87
  18.0 0.7 fusion.85
  18.8 3.9 %gather_fusion = bf16[1024,256]{1,0:T(8,128)(2,1)S(1)} fusion(bf16[256,64]{0,1:T(8,128)(2,1)S(1)} %copy-done.1, s32[1024]{0:T(1024)S(1)} %get-tuple-element.395), kind=kCustom, calls=%fused_computation.2.clone.clone.1 | custom fusion | bytes 1052672 | tf_op jit(solution)/shard_map/while/body/eval_jaxpr/jit(_take)/gather | solution.py:44
  22.7 3.9 %gather_fusion.1 = bf16[1024,256]{1,0:T(8,128)(2,1)S(1)} fusion(bf16[256,64]{0,1:T(8,128)(2,1)S(1)} %copy-done.1, s32[1024]{0:T(1024)S(1)} %get-tuple-element.396), kind=kCustom, calls=%fused_computation.clone.clone.1 | custom fusion | bytes 1052672 | tf_op jit(solution)/shard_map/while/body/eval_jaxpr/jit(_take)/gather | solution.py:43
  26.6 0.7 fusion.86
  27.4 0.7 dynamic_slice.128
  28.1 1.1 fusion.87
  29.2 0.7 fusion.85
  30.0 3.9 %gather_fusion = bf16[1024,256]{1,0:T(8,128)(2,1)S(1)} fusion(bf16[256,64]{0,1:T(8,128)(2,1)S(1)} %copy-done.1, s32[1024]{0:T(1024)S(1)} %get-tuple-element.395), kind=kCustom, calls=%fused_computation.2.clone.clone.1 | custom fusion | bytes 1052672 | tf_op jit(solution)/shard_map/while/body/eval_jaxpr/jit(_take)/gather | solution.py:44
  33.9 3.9 %gather_fusion.1 = bf16[1024,256]{1,0:T(8,128)(2,1)S(1)} fusion(bf16[256,64]{0,1:T(8,128)(2,1)S(1)} %copy-done.1, s32[1024]{0:T(1024)S(1)} %get-tuple-element.396), kind=kCustom, calls=%fused_computation.clone.clone.1 | custom fusion | bytes 1052672 | tf_op jit(solution)/shard_map/while/body/eval_jaxpr/jit(_take)/gather | solution.py:43
  37.9 0.7 fusion.86
  38.6 0.7 dynamic_slice.128
  39.3 1.1 fusion.87
  40.5 0.5 reshape.156
  41.0 0.8 copy.26
  41.7 7.4 %all-to-all-start = ((bf16[8,260,64]{1,2,0:T(8,128)(2,1)}), bf16[8,260,64]{1,2,0:T(8,128)(2,1)S(1)}, u32[]{:S(2)}, u32[]{:S(2)}) async-start(bf16[8,260,64]{1,2,0:T(8,128)(2,1)} %copy.26), calls=%async_computation | async-start | bytes 786432 | tf_op jit(solution)/shard_map/all_to_all | solution.py:143
  49.3 1.8 %all_gather.10 = bf16[2,10,64]{2,0,1:T(2,128)(2,1)S(1)} all-gather(bf16[2,5,64]{2,0,1:T(2,128)(2,1)S(1)} %broadcast_select_fusion), channel_id=1, replica_groups=mesh['groups'=2,'wide'=8,'narrow'=2] {'narrow'}, dimensions={1}, use_global_device_ids=true | all-gather | bytes 3840 | tf_op jit(solution)/shard_map/all_gather | solution.py:162
  51.2 21.8 %all-reduce.1 = f32[8]{0:T(128)S(1)} all-reduce(f32[8]{0:T(128)S(1)} %get-tuple-element.337), channel_id=1, replica_groups=mesh['groups'=2,'wide'=8,'narrow'=2] {'wide'}, use_global_device_ids=true, to_apply=%add.1 | all-reduce | flops 8 | bytes 64
  73.0 0.2 reduce-window.21
  73.2 0.1 copy.31
  73.3 4.8 %gather_fusion.4 = bf16[2080,10]{1,0:T(8,128)(2,1)S(1)} fusion(bf16[10,64]{0,1:T(8,128)(2,1)S(1)} %bitcast.90, s32[3072]{0:T(1024)S(1)} %pad_clamp_fusion.1), kind=kCustom, calls=%fused_computation.1.clone | custom fusion | bytes 91520 | tf_op jit(solution)/shard_map/jit(_take)/gather | solution.py:43
  78.1 4.8 %gather_fusion.5 = bf16[2080,10]{1,0:T(8,128)(2,1)S(1)} fusion(bf16[10,64]{0,1:T(8,128)(2,1)S(1)} %bitcast.91, s32[3072]{0:T(1024)S(1)} %pad_clamp_fusion), kind=kCustom, calls=%fused_computation.5.clone | custom fusion | bytes 91520 | tf_op jit(solution)/shard_map/jit(_take)/gather | solution.py:44
  82.9 0.6 dynamic-slice.1
  84.2 0.9 convolution_convert_fusion.1
  85.2 0.2 copy.32
  85.4 33.2 %all-gather = bf16[1,2080,64]{2,0,1:T(2,128)(2,1)S(1)} all-gather(bf16[1,260,64]{2,0,1:T(2,128)(2,1)S(1)} %copy.32), channel_id=2, replica_groups=mesh['groups'=2,'wide'=8,'narrow'=2] {'wide'}, dimensions={1}, use_global_device_ids=true | all-gather | bytes 299520 | tf_op jit(solution)/shard_map/all_gather | solution.py:165
  118.6 1.3 copy.33
  119.9 0.8 copy.28
  120.7 3.5 %all-to-all-start.1 = ((bf16[8,260,64]{1,2,0:T(8,128)(2,1)}), bf16[8,260,64]{1,2,0:T(8,128)(2,1)S(1)}, u32[]{:S(2)}, u32[]{:S(2)}) async-start(bf16[8,260,64]{1,2,0:T(8,128)(2,1)} %copy.28), calls=%async_computation.1 | async-start | bytes 786432 | tf_op jit(solution)/shard_map/all_to_all | solution.py:151
  124.2 0.6 fusion.42
  124.8 2.5 %all-reduce.2 = f32[10,64]{1,0:T(8,128)S(1)} all-reduce(f32[10,64]{1,0:T(8,128)S(1)} %fusion.42), channel_id=3, replica_groups=mesh['groups'=2,'wide'=8,'narrow'=2] {'narrow'}, use_global_device_ids=true, to_apply=%region_8.11.clone | all-reduce | flops 640 | bytes 5120
  127.3 0.1 multiply_reduce_fusion.1
  127.4 0.7 multiply_convert_fusion.8
  128.0 5.3 %all-to-all-done.1 = bf16[8,260,64]{1,2,0:T(8,128)(2,1)S(1)} async-done(((bf16[8,260,64]{1,2,0:T(8,128)(2,1)}), bf16[8,260,64]{1,2,0:T(8,128)(2,1)S(1)}, u32[]{:S(2)}, u32[]{:S(2)}) %all-to-all-start.1) | async-done | bytes 266272 | tf_op jit(solution)/shard_map/all_to_all | solution.py:151
  133.3 0.2 copy.29
  133.5 0.3 reshape.157
  133.9 27.9 %while.30 = (s32[]{:T(128)}, f32[256,64]{0,1:T(8,128)S(1)}, bf16[256,64]{0,1:T(8,128)(2,1)S(1)}, bf16[3072,64]{0,1:T(8,128)(2,1)S(1)}, s32[]{:T(128)}, /*index=5...) while((s32[]{:T(128)}, f32[256,64]{0,1:T(8,128)S(1)}, ...), condition=%wide.region_6.8_spmd.clone.clone, body=%wide.region_5.7_spmd.sunk.clone.clone.sunk | while | flops 35442696 | bytes 3457205 | solution.py:88
  134.0 3.9 %gather_fusion.2 = bf16[1024,256]{1,0:T(8,128)(2,1)S(1)} fusion(bf16[256,64]{0,1:T(8,128)(2,1)S(1)} %get-tuple-element.464, s32[1024]{0:T(1024)S(1)} %get-tuple-element.403), kind=kCustom, calls=%fused_computation.4.clone.clone.1 | custom fusion | bytes 1052672 | tf_op jit(solution)/shard_map/while/body/eval_jaxpr/jit(_take)/gather | solution.py:44
  137.9 3.9 %gather_fusion.3 = bf16[1024,256]{1,0:T(8,128)(2,1)S(1)} fusion(bf16[256,64]{0,1:T(8,128)(2,1)S(1)} %get-tuple-element.464, s32[1024]{0:T(1024)S(1)} %get-tuple-element.404), kind=kCustom, calls=%fused_computation.3.clone.clone.1 | custom fusion | bytes 1052672 | tf_op jit(solution)/shard_map/while/body/eval_jaxpr/jit(_take)/gather | solution.py:43
  141.9 0.7 dynamic_slice.132
  142.6 0.6 convolution_add_fusion.2
  143.3 3.9 %gather_fusion.2 = bf16[1024,256]{1,0:T(8,128)(2,1)S(1)} fusion(bf16[256,64]{0,1:T(8,128)(2,1)S(1)} %get-tuple-element.464, s32[1024]{0:T(1024)S(1)} %get-tuple-element.403), kind=kCustom, calls=%fused_computation.4.clone.clone.1 | custom fusion | bytes 1052672 | tf_op jit(solution)/shard_map/while/body/eval_jaxpr/jit(_take)/gather | solution.py:44
  147.2 3.9 %gather_fusion.3 = bf16[1024,256]{1,0:T(8,128)(2,1)S(1)} fusion(bf16[256,64]{0,1:T(8,128)(2,1)S(1)} %get-tuple-element.464, s32[1024]{0:T(1024)S(1)} %get-tuple-element.404), kind=kCustom, calls=%fused_computation.3.clone.clone.1 | custom fusion | bytes 1052672 | tf_op jit(solution)/shard_map/while/body/eval_jaxpr/jit(_take)/gather | solution.py:43
  151.2 0.7 dynamic_slice.132
  151.9 0.6 convolution_add_fusion.2
  152.6 3.9 %gather_fusion.2 = bf16[1024,256]{1,0:T(8,128)(2,1)S(1)} fusion(bf16[256,64]{0,1:T(8,128)(2,1)S(1)} %get-tuple-element.464, s32[1024]{0:T(1024)S(1)} %get-tuple-element.403), kind=kCustom, calls=%fused_computation.4.clone.clone.1 | custom fusion | bytes 1052672 | tf_op jit(solution)/shard_map/while/body/eval_jaxpr/jit(_take)/gather | solution.py:44
  156.5 3.9 %gather_fusion.3 = bf16[1024,256]{1,0:T(8,128)(2,1)S(1)} fusion(bf16[256,64]{0,1:T(8,128)(2,1)S(1)} %get-tuple-element.464, s32[1024]{0:T(1024)S(1)} %get-tuple-element.404), kind=kCustom, calls=%fused_computation.3.clone.clone.1 | custom fusion | bytes 1052672 | tf_op jit(solution)/shard_map/while/body/eval_jaxpr/jit(_take)/gather | solution.py:43
  160.5 0.7 dynamic_slice.132
  161.2 0.6 convolution_add_fusion.2
  161.9 0.4 multiply_reduce_fusion
  162.3 0.6 fusion.55
  (55 shorter events, 1.0 us)
Async XLA Ops:
  6.8 0.8 copy-start.1
  18.0 0.8 copy-start.1
  29.2 0.8 copy-start.1
  40.4 8.7 %copy-start.9 = (s32[5]{0:T(128)S(1)}, s32[5]{0:T(128)}, u32[]{:S(2)}) copy-start(s32[5]{0:T(128)} %param.25) | copy-start | bytes 64
  40.4 8.8 %copy-start.8 = (bf16[5,64]{1,0:T(8,128)(2,1)S(1)}, bf16[5,64]{1,0:T(8,128)(2,1)}, u32[]{:S(2)}) copy-start(bf16[5,64]{1,0:T(8,128)(2,1)} %param.24) | copy-start | bytes 1924
  40.5 32.8 %copy-start.7 = (s32[2080]{0:T(1024)S(1)}, s32[2080]{0:T(1024)}, u32[]{:S(2)}) copy-start(s32[2080]{0:T(1024)} %constant.170) | copy-start | bytes 24964
  40.9 37.1 %copy-start.6 = (s32[2080]{0:T(1024)S(1)}, s32[2080]{0:T(1024)}, u32[]{:S(2)}) copy-start(s32[2080]{0:T(1024)} %constant.171) | copy-start | bytes 24964
  41.7 41.1 %copy-start.11 = (u32[32]{0:T(128)S(1)}, u32[32]{0:T(128)}, u32[]{:S(2)}) copy-start(u32[32]{0:T(128)} %constant.174) | copy-start | bytes 388
  41.7 42.5 %all-to-all-start = ((bf16[8,260,64]{1,2,0:T(8,128)(2,1)}), bf16[8,260,64]{1,2,0:T(8,128)(2,1)S(1)}, u32[]{:S(2)}, u32[]{:S(2)}) async-start(bf16[8,260,64]{1,2,0:T(8,128)(2,1)} %copy.26), calls=%async_computation | async-start | bytes 786432 | tf_op jit(solution)/shard_map/all_to_all | solution.py:143
  119.9 4.3 %copy-start.10 = (f32[2080]{0:T(1024)S(1)}, f32[2080]{0:T(1024)}, u32[]{:S(2)}) copy-start(f32[2080]{0:T(1024)} %constant.145) | copy-start | bytes 24964
  120.7 12.6 %all-to-all-start.1 = ((bf16[8,260,64]{1,2,0:T(8,128)(2,1)}), bf16[8,260,64]{1,2,0:T(8,128)(2,1)S(1)}, u32[]{:S(2)}, u32[]{:S(2)}) async-start(bf16[8,260,64]{1,2,0:T(8,128)(2,1)} %copy.28), calls=%async_computation.1 | async-start | bytes 786432 | tf_op jit(solution)/shard_map/all_to_all | solution.py:151
  128.0 5.8 %copy-start = (bf16[1,256,64]{1,2,0:T(8,128)(2,1)S(1)}, bf16[1,256,64]{1,2,0:T(8,128)(2,1)}, u32[]{:S(2)}) copy-start(bf16[1,256,64]{1,2,0:T(8,128)(2,1)} %param.19) | copy-start | bytes 98308
  128.0 5.8 %copy-start.3 = (s32[3072]{0:T(1024)S(1)}, s32[3072]{0:T(1024)}, u32[]{:S(2)}) copy-start(s32[3072]{0:T(1024)} %get-tuple-element.477) | copy-start | bytes 36868
  128.0 5.8 %copy-start.4 = (s32[3072]{0:T(1024)S(1)}, s32[3072]{0:T(1024)}, u32[]{:S(2)}) copy-start(s32[3072]{0:T(1024)} %get-tuple-element.478) | copy-start | bytes 36868
  133.9 27.9 %copy-start.2 = (bf16[256,64]{0,1:T(8,128)(2,1)S(1)}, bf16[256,64]{0,1:T(8,128)(2,1)}, u32[]{:S(2)}) copy-start(bf16[256,64]{0,1:T(8,128)(2,1)} %get-tuple-element.474) | copy-start | bytes 98308
  133.9 27.9 %copy-start.5 = (bf16[1,256,64]{1,2,0:T(8,128)(2,1)S(1)}, bf16[1,256,64]{1,2,0:T(8,128)(2,1)}, u32[]{:S(2)}) copy-start(bf16[1,256,64]{1,2,0:T(8,128)(2,1)} %param.21) | copy-start | bytes 98308
where the time goes:
time: 164 us; the launch traced here: 163 us
  local copies, waits for them, and re-layouts  69.6 us (42%)
  blocking collectives  59.3 us (36%)
  starting transfers between devices  10.9 us (7%)
  other arithmetic  8.08 us (5%)
  matrix products  7.18 us (4%)
  waiting for transfers between devices  5.25 us (3%)
  between operations  2.25 us (1%)
    all_gather x1, blocking collectives, on_device(): shard_portion = lax.all_gather(final_slice, 'wide', axis=0, tiled=True)  33.2 us
    gather x7, local copies, waits for them, and re-layouts, pair_block(): leading_columns = jnp.take(rows, lead_part, axis=1).astype(jnp.float32)  28.4 us
    gather x7, local copies, waits for them, and re-layouts, pair_block(): right_cols = jnp.take(rows, trail_part, axis=1).astype(jnp.float32)  28.4 us
    unnamed x2, blocking collectives  24.3 us
    all_to_all x1, starting transfers between devices, on_device(): lax.all_to_all(span_state.reshape(wide_count, rows_per, head_width), 'wid...  7.41 us
    all_to_all x1, waiting for transfers between devices, on_device(): lax.all_to_all(rounded[:wide_count], 'wide', split_axis=0, concat_axis=0,...  5.25 us
    unnamed x27, local copies, waits for them, and re-layouts  4.03 us
    all_to_all x1, starting transfers between devices, on_device(): lax.all_to_all(rounded[:wide_count], 'wide', split_axis=0, concat_axis=0,...  3.45 us
  transfers between devices with their start and end apart: 2, of which 1 were waited for; matrix products, arithmetic and copies ran while one was open for 7% of the time, Pallas kernels for 0%

commit v1 on v0

--- a/solution.py
+++ b/solution.py
@@ -1,7 +1,11 @@
+import functools
+
 import jax
 import jax.numpy as jnp
 import numpy as np
 from jax import lax
+from jax.experimental import pallas as pl
+from jax.experimental.pallas import tpu as pltpu
 from jax.sharding import PartitionSpec as P
 
 epsilon = 1e-06
@@ -176,6 +180,268 @@
     return (prompt_out[None], cont_out)
 
 
+def flip(place, bits):
+    for bit in (1, 2):
+        if bits & bit:
+            place = place + bit - 2 * bit * ((place // bit) % 2)
+    return place
+
+
+def triple(rows):
+    high = rows.astype(jnp.bfloat16)
+    rest = rows - high.astype(jnp.float32)
+    middle = rest.astype(jnp.bfloat16)
+    low = (rest - middle.astype(jnp.float32)).astype(jnp.bfloat16)
+    return high, middle, low
+
+
+def prefix_sums(rows, upper):
+    high, middle, low = triple(rows)
+    add = lambda part: jnp.dot(part, upper, preferred_element_type=jnp.float32)
+    return add(high) + add(middle) + add(low)
+
+
+def gather_kernel(
+    n,
+    lengths_ref,
+    prompt_ref,
+    query_ref,
+    key_ref,
+    value_ref,
+    gate_ref,
+    cont_ref,
+    out_ref,
+    cont_out_ref,
+    kv,
+    gates,
+    queries,
+    cont_own,
+    cont_other,
+    scale_carried,
+    scale_final,
+    carried,
+    reach_out,
+    reach_in,
+    gate_send,
+    gate_recv,
+    col_send,
+    x_send,
+    kv_recv,
+    pair_send,
+    pair_recv,
+):
+    f32, bf16 = jnp.float32, jnp.bfloat16
+    me = lax.axis_index("wide")
+    lane = lax.axis_index("narrow")
+    row, side = me // 2, me % 2
+    levels = n // 2
+    tok, width = query_ref.shape[1], query_ref.shape[2]
+    cont_count = cont_ref.shape[0]
+    cont_pad = cont_own.shape[0]
+    mesh_id = pl.DeviceIdType.MESH
+    peer_x = me + 1 - 2 * side
+    sibling = 1 - lane
+    order = {2: (1,), 4: (1, 3, 2)}[levels]
+
+    barrier = pltpu.get_barrier_semaphore()
+    for step in range(1, n):
+        pl.semaphore_signal(
+            barrier, inc=1, device_id={"wide": (me + step) % n}, device_id_type=mesh_id
+        )
+    pl.semaphore_signal(barrier, inc=1, device_id={"narrow": sibling}, device_id_type=mesh_id)
+
+    kv[me] = jnp.concatenate([value_ref[0], key_ref[0]], axis=1)
+    gates[me] = gate_ref[...]
+    queries[:tok] = jnp.concatenate([jnp.zeros((tok, width), bf16), query_ref[0]], axis=1)
+    cont_own[...] = jnp.zeros_like(cont_own)
+    cont_own[:cont_count] = jnp.concatenate(
+        [jnp.zeros((cont_count, width), bf16), cont_ref[...]], axis=1
+    )
+
+    def send(src, dst, send_sem, recv_sem, where):
+        return pltpu.make_async_remote_copy(
+            src_ref=src,
+            dst_ref=dst,
+            send_sem=send_sem,
+            recv_sem=recv_sem,
+            device_id=where,
+            device_id_type=mesh_id,
+        )
+
+    pl.semaphore_wait(barrier, n)
+
+    gate_copies = []
+    for step in range(1, n):
+        to = (me + step) % n
+        gate_copies.append(
+            send(gate_ref, gates.at[me], gate_send.at[step], gate_recv.at[step], {"wide": to})
+        )
+    kv_copies = []
+    for bits in tuple(reversed(sorted(order))):
+        to = 2 * flip(row, bits) + side
+        kv_copies.append(
+            send(kv.at[me], kv.at[me], col_send.at[bits], kv_recv.at[me], {"wide": to})
+        )
+    kv_copies.append(send(kv.at[me], kv.at[me], x_send.at[0], kv_recv.at[me], {"wide": peer_x}))
+    cont_copy = send(
+        cont_own, cont_other, pair_send.at[0], pair_recv.at[0], {"narrow": sibling}
+    )
+    for copy in gate_copies:
+        copy.start()
+    for copy in kv_copies:
+        copy.start()
+    cont_copy.start()
+
+    def wait_block(block):
+        send(
+            kv.at[block], kv.at[block], x_send.at[0], kv_recv.at[block], {"wide": peer_x}
+        ).wait_recv()
+
+    def forward(block, bits):
+        copy = send(
+            kv.at[block], kv.at[block], x_send.at[bits], kv_recv.at[block], {"wide": peer_x}
+        )
+        copy.start()
+        return copy
+
+    length = lengths_ref[0]
+    down = lax.broadcasted_iota(jnp.int32, (tok, tok), 0)
+    across = lax.broadcasted_iota(jnp.int32, (tok, tok), 1)
+    upper = (down <= across).astype(bf16)
+    lower = across <= down
+    start = me * tok
+    live_row = (start + lax.broadcasted_iota(jnp.int32, (1, tok), 1)) < length
+    live_col = (start + lax.broadcasted_iota(jnp.int32, (tok, 1), 0)) < length
+    gate_row = jnp.where(live_row, gate_ref[...], 0.0)
+    total_col = jnp.sum(jnp.where(lower, gate_row, 0.0), axis=1, keepdims=True)
+    total_row = prefix_sums(jnp.broadcast_to(gate_row, (8, tok)), upper)[:1]
+    contract = (((1,), (1,)), ((), ()))
+    own = kv[me]
+    scores = lax.dot_general(queries[:tok], own, contract, preferred_element_type=f32)
+    decay = jnp.exp(jnp.where(lower & live_row, total_col - total_row, -jnp.inf))
+    local = jnp.dot((scores * scores * decay).astype(bf16), own, preferred_element_type=f32)
+
+    for step in range(1, n):
+        block = (me + n - step) % n
+        send(
+            gate_ref, gates.at[block], gate_send.at[step], gate_recv.at[step], {"wide": block}
+        ).wait_recv()
+    gate_all = jnp.concatenate([gates[u] for u in range(n)], axis=0)
+    block_id = lax.broadcasted_iota(jnp.int32, (n, tok), 0)
+    live_all = block_id * tok + lax.broadcasted_iota(jnp.int32, (n, tok), 1) < length
+    sums = prefix_sums(jnp.where(live_all, gate_all, 0.0), upper)
+    ends = sums[:, tok - 1 :]
+    rest = ends - sums
+    to_me = rest
+    to_end = rest
+    for v in range(1, n):
+        end_v = jnp.where(block_id < v, ends[v : v + 1], 0.0)
+        to_end = to_end + end_v
+        to_me = to_me + jnp.where(v < me, end_v, 0.0)
+    to_me = jnp.exp(jnp.where(live_all & (block_id < me), to_me, -jnp.inf))
+    to_end = jnp.exp(jnp.where(live_all, to_end, -jnp.inf))
+    for u in range(n):
+        scale_carried[u] = to_me[u : u + 1]
+        scale_final[u] = to_end[u : u + 1]
+
+    cont_copy.wait()
+    queries[tok : tok + cont_pad] = cont_own[...]
+    queries[tok + cont_pad :] = cont_other[...]
+
+    cont_scores = lax.dot_general(queries[tok:], own, contract, preferred_element_type=f32)
+    cont_weights = (cont_scores * cont_scores * scale_final[me]).astype(bf16)
+    carried[:tok] = jnp.zeros((tok, 2 * width), f32)
+    carried[tok:] = jnp.dot(cont_weights, own, preferred_element_type=f32)
+
+    def add_block(block):
+        lines = kv[block]
+        scores = lax.dot_general(queries[...], lines, contract, preferred_element_type=f32)
+        scores = scores * scores
+        weights = jnp.concatenate(
+            [scores[:tok] * scale_carried[block], scores[tok:] * scale_final[block]], axis=0
+        ).astype(bf16)
+        carried[...] += jnp.dot(weights, lines, preferred_element_type=f32)
+
+    forwards = []
+    wait_block(peer_x)
+    add_block(peer_x)
+    for bits in order:
+        block = 2 * flip(row, bits) + side
+        wait_block(block)
+        forwards.append(forward(block, bits))
+        add_block(block)
+    for bits in order:
+        block = 2 * flip(row, bits) + 1 - side
+        wait_block(block)
+        add_block(block)
+
+    reach_out[...] = carried[tok + cont_pad :]
+    reach_copy = send(
+        reach_out, reach_in, pair_send.at[1], pair_recv.at[1], {"narrow": sibling}
+    )
+    reach_copy.start()
+
+    def rms(rows):
+        rows = rows[:, :width]
+        square = jnp.sum(rows * rows, axis=1, keepdims=True) * (1.0 / width)
+        return rows * lax.rsqrt(square + epsilon)
+
+    result = rms(local + jnp.exp(total_col) * carried[:tok])
+    out_ref[0] = jnp.where(live_col, result, 0.0).astype(bf16)
+
+    row_id = lax.broadcasted_iota(jnp.int32, (cont_pad, 2 * width), 0)
+    prompts = jnp.zeros((cont_pad, 2 * width), jnp.int32)
+    for r in range(cont_count):
+        prompts = jnp.where(row_id == r, prompt_ref[r], prompts)
+    reach_copy.wait()
+    reach = jnp.where(prompts == lane, carried[tok : tok + cont_pad], reach_in[...])
+    cont_out_ref[...] = rms(reach)[:cont_count].astype(bf16)
+
+    for copy in gate_copies + kv_copies + forwards:
+        copy.wait_send()
+
+
+def gathered(n, queries, key_rows, values, log_gate, lengths, cont_queries, cont_prompt):
+    tok, width = queries.shape[1], queries.shape[2]
+    cont_count = cont_queries.shape[0]
+    cont_pad = -(-cont_count // 16) * 16
+    levels = n // 2
+    vmem = pl.BlockSpec(memory_space=pltpu.VMEM)
+    smem = pl.BlockSpec(memory_space=pltpu.SMEM)
+    dma = lambda count: pltpu.SemaphoreType.DMA((count,))
+    f32, bf16 = jnp.float32, jnp.bfloat16
+    return pl.pallas_call(
+        functools.partial(gather_kernel, n),
+        name="retention",
+        out_shape=(
+            jax.ShapeDtypeStruct((1, tok, width), bf16),
+            jax.ShapeDtypeStruct((cont_count, width), bf16),
+        ),
+        in_specs=[smem, smem, vmem, vmem, vmem, vmem, vmem],
+        out_specs=(vmem, vmem),
+        scratch_shapes=[
+            pltpu.VMEM((n, tok, 2 * width), bf16),
+            pltpu.VMEM((n, 1, tok), f32),
+            pltpu.VMEM((tok + 2 * cont_pad, 2 * width), bf16),
+            pltpu.VMEM((cont_pad, 2 * width), bf16),
+            pltpu.VMEM((cont_pad, 2 * width), bf16),
+            pltpu.VMEM((n, 1, tok), f32),
+            pltpu.VMEM((n, 1, tok), f32),
+            pltpu.VMEM((tok + 2 * cont_pad, 2 * width), f32),
+            pltpu.VMEM((cont_pad, 2 * width), f32),
+            pltpu.VMEM((cont_pad, 2 * width), f32),
+            dma(n),
+            dma(n),
+            dma(levels),
+            dma(levels),
+            dma(n),
+            dma(2),
+            dma(2),
+        ],
+        compiler_params=pltpu.CompilerParams(collective_id=0, has_side_effects=True),
+    )(lengths, cont_prompt, queries, key_rows, values, log_gate, cont_queries)
+
+
 def solution(mesh):
     in_specs = (
         P(("groups", "narrow"), "wide", None),
@@ -187,6 +453,9 @@
         P(("groups", "wide", "narrow")),
     )
     out_specs = (P(("groups", "narrow"), "wide", None), P(("groups", "wide", "narrow"), None))
+    wide_count = mesh.shape["wide"]
+    direct = mesh.shape["narrow"] == 2 and wide_count in (4, 8)
+    program = functools.partial(gathered, wide_count) if direct else on_device
     return jax.shard_map(
-        on_device, mesh=mesh, in_specs=in_specs, out_specs=out_specs, check_vma=False
-    )
+        program, mesh=mesh, in_specs=in_specs, out_specs=out_specs, check_vma=False
+    )

time: 164 us -> 25.6 us (0.16)
  local copies, waits for them, and re-layouts: 69.6 us -> 5.09 us
  blocking collectives: 59.3 us -> 0 us
  Pallas kernels: 0 us -> 18.9 us
  starting transfers between devices: 10.9 us -> 0 us
  other arithmetic: 8.08 us -> 0 us
  matrix products: 7.18 us -> 0 us
  waiting for transfers between devices: 5.25 us -> 0 us
    gather x14 -> x0, local copies, waits for them, and re-layouts: 56.8 us -> none  [the longest x7 28.4 us: pair_block(): leading_columns = jnp.take(rows, lead_part, axis=1).astype(jnp.float32)]
    all_gather x2 -> x0, blocking collectives: 35 us -> none  [the longest x1 33.2 us: on_device(): shard_portion = lax.all_gather(final_slice, 'wide', axis=0, tiled=True)]
    unnamed x2 -> x0, blocking collectives: 24.3 us -> none
    pallas_call x0 -> x1, Pallas kernels: none -> 18.9 us  [gathered(): pl.pallas_call(functools.partial(gather_kernel, n), name='retention', out...]
    all_to_all x2 -> x0, starting transfers between devices: 10.9 us -> none  [the longest x1 7.41 us: on_device(): lax.all_to_all(span_state.reshape(wide_count, rows_per, head_width), 'wid...]
    dot_general x9 -> x0, matrix products: 7.18 us -> none  [the longest x3 3.38 us: fill_block(): lax.dot_general(features, spread, (((0,), (0,)), ((), ())), preferred_ele...]
    all_to_all x2 -> x0, waiting for transfers between devices: 5.25 us -> none  [the longest x1 5.25 us: on_device(): lax.all_to_all(rounded[:wide_count], 'wide', split_axis=0, concat_axis=0,...]
    dynamic_slice x8 -> x0, local copies, waits for them, and re-layouts: 4.27 us -> none  [the longest x3 2.09 us: add_block(): lax.dynamic_slice_in_dim(doubled_all, first_row, block_width)]
  transfers between devices with their start and end apart: 2 -> 0, of which waited for: 1 -> 0; matrix products, arithmetic and copies ran while one was open for 7% -> 0% of each run, Pallas kernels for 0% -> 0%
where the time goes in v1:
time: 25.6 us; the launch traced here: 25.3 us
  Pallas kernels  18.9 us (74%)
  local copies, waits for them, and re-layouts  5.09 us (20%)
  between operations  1.3 us (5%)
    pallas_call x1, Pallas kernels, gathered(): pl.pallas_call(functools.partial(gather_kernel, n), name='retention', out...  18.9 us
    unnamed x10, local copies, waits for them, and re-layouts  3.55 us
    pallas_call x1, local copies, waits for them, and re-layouts, gathered(): pl.pallas_call(functools.partial(gather_kernel, n), name='retention', out...  1.54 us

profile of v1, /device:TPU:0, one launch (start us, length us, event | category | flops | bytes accessed | tf_op | source)
XLA Modules:
  0.0 25.3 jit_solution(2028816337031591195)
XLA Ops:
  1.3 0.0 copy-start
  1.3 1.5 %copy.9.query_ref = bf16[1,256,64]{2,1,0:T(8,128)(2,1)} copy(bf16[1,256,64]{1,2,0:T(8,128)(2,1)} %param.7) | data formatting | bytes 65536 | tf_op args[0]
  2.8 0.0 copy-done
  2.8 0.0 copy-start.1
  2.8 0.7 %copy.10.key_ref = bf16[1,256,64]{2,1,0:T(8,128)(2,1)} copy(bf16[1,256,64]{1,2,0:T(8,128)(2,1)S(1)} %copy-done) | data formatting | bytes 65536 | tf_op args[1]
  3.5 0.0 copy-done.1
  3.5 0.7 %copy.11.value_ref = bf16[1,256,64]{2,1,0:T(8,128)(2,1)} copy(bf16[1,256,64]{1,2,0:T(8,128)(2,1)S(1)} %copy-done.1) | data formatting | bytes 65536 | tf_op args[2]
  4.3 18.9 %retention.1 = (bf16[1,256,64]{2,1,0:T(8,128)(2,1)}, bf16[5,64]{1,0:T(8,128)(2,1)}) custom-call(s32[1]{0:T(128)S(6)} %copy.14.lengths_ref, s32[5]{0:T(128)} %prompt_ref.1, bf16[1,256,64]{2,1,0:T(8,128)(2,1)} %copy.9.query_ref, bf16[1,256,64]{2,1,0:T(8,128)(2,1)} %copy.10.key_ref, bf16[1,256,64]{2,1,0:T(8,128)(2,1)} %copy.11.value_ref, f32[1,256]{1,0:T(1,128)} %gate_ref.1, ...), custom_call_target="tpu_custom_call" | custom-call | tf_op jit(solution)/shard_map/retention/pallas_call | solution.py:413
  23.2 0.0 copy-start.2
  23.2 1.5 %copy.12 = bf16[1,256,64]{1,2,0:T(8,128)(2,1)} copy(bf16[1,256,64]{2,1,0:T(8,128)(2,1)} %get-tuple-element.2) | data formatting | bytes 65536 | tf_op jit(solution)/shard_map/retention/pallas_call | solution.py:413
  24.7 0.0 copy-done.2
  24.7 0.6 %copy.15 = bf16[5,64]{1,0:T(8,128)(2,1)} copy(bf16[5,64]{1,0:T(8,128)(2,1)S(1)} %copy-done.2) | data formatting | bytes 1280
Async XLA Ops:
  1.3 1.5 %copy-start = (bf16[1,256,64]{1,2,0:T(8,128)(2,1)S(1)}, bf16[1,256,64]{1,2,0:T(8,128)(2,1)}, u32[]{:S(2)}) copy-start(bf16[1,256,64]{1,2,0:T(8,128)(2,1)} %param.8) | copy-start | bytes 98308
  2.8 0.8 %copy-start.1 = (bf16[1,256,64]{1,2,0:T(8,128)(2,1)S(1)}, bf16[1,256,64]{1,2,0:T(8,128)(2,1)}, u32[]{:S(2)}) copy-start(bf16[1,256,64]{1,2,0:T(8,128)(2,1)} %param.9) | copy-start | bytes 98308
  23.2 1.6 %copy-start.2 = (bf16[5,64]{1,0:T(8,128)(2,1)S(1)}, bf16[5,64]{1,0:T(8,128)(2,1)}, u32[]{:S(2)}) copy-start(bf16[5,64]{1,0:T(8,128)(2,1)} %get-tuple-element.7) | copy-start | bytes 1924

commit v2 on v1

--- a/solution.py
+++ b/solution.py
@@ -235,7 +235,7 @@
     lane = lax.axis_index("narrow")
     row, side = me // 2, me % 2
     levels = n // 2
-    tok, width = query_ref.shape[1], query_ref.shape[2]
+    width, tok = query_ref.shape[1], query_ref.shape[2]
     cont_count = cont_ref.shape[0]
     cont_pad = cont_own.shape[0]
     mesh_id = pl.DeviceIdType.MESH
@@ -250,13 +250,11 @@
         )
     pl.semaphore_signal(barrier, inc=1, device_id={"narrow": sibling}, device_id_type=mesh_id)
 
-    kv[me] = jnp.concatenate([value_ref[0], key_ref[0]], axis=1)
+    kv[me] = jnp.concatenate([value_ref[0], key_ref[0]], axis=0)
     gates[me] = gate_ref[...]
-    queries[:tok] = jnp.concatenate([jnp.zeros((tok, width), bf16), query_ref[0]], axis=1)
+    queries[:tok] = jnp.transpose(query_ref[0])
     cont_own[...] = jnp.zeros_like(cont_own)
-    cont_own[:cont_count] = jnp.concatenate(
-        [jnp.zeros((cont_count, width), bf16), cont_ref[...]], axis=1
-    )
+    cont_own[:cont_count, :width] = cont_ref[...]
 
     def send(src, dst, send_sem, recv_sem, where):
         return pltpu.make_async_remote_copy(
@@ -311,15 +309,15 @@
     lower = across <= down
     start = me * tok
     live_row = (start + lax.broadcasted_iota(jnp.int32, (1, tok), 1)) < length
-    live_col = (start + lax.broadcasted_iota(jnp.int32, (tok, 1), 0)) < length
     gate_row = jnp.where(live_row, gate_ref[...], 0.0)
     total_col = jnp.sum(jnp.where(lower, gate_row, 0.0), axis=1, keepdims=True)
     total_row = prefix_sums(jnp.broadcast_to(gate_row, (8, tok)), upper)[:1]
     contract = (((1,), (1,)), ((), ()))
-    own = kv[me]
-    scores = lax.dot_general(queries[:tok], own, contract, preferred_element_type=f32)
+    scores = jnp.dot(queries[:tok], key_ref[0], preferred_element_type=f32)
     decay = jnp.exp(jnp.where(lower & live_row, total_col - total_row, -jnp.inf))
-    local = jnp.dot((scores * scores * decay).astype(bf16), own, preferred_element_type=f32)
+    local = lax.dot_general(
+        (scores * scores * decay).astype(bf16), value_ref[0], contract, preferred_element_type=f32
+    )
 
     for step in range(1, n):
         block = (me + n - step) % n
@@ -345,22 +343,25 @@
         scale_final[u] = to_end[u : u + 1]
 
     cont_copy.wait()
-    queries[tok : tok + cont_pad] = cont_own[...]
-    queries[tok + cont_pad :] = cont_other[...]
-
-    cont_scores = lax.dot_general(queries[tok:], own, contract, preferred_element_type=f32)
+    queries[tok : tok + cont_pad] = cont_own[:, :width]
+    queries[tok + cont_pad :] = cont_other[:, :width]
+
+    cont_scores = jnp.dot(queries[tok:], key_ref[0], preferred_element_type=f32)
     cont_weights = (cont_scores * cont_scores * scale_final[me]).astype(bf16)
-    carried[:tok] = jnp.zeros((tok, 2 * width), f32)
-    carried[tok:] = jnp.dot(cont_weights, own, preferred_element_type=f32)
+    carried[:tok] = jnp.zeros((tok, width), f32)
+    carried[tok:] = lax.dot_general(
+        cont_weights, value_ref[0], contract, preferred_element_type=f32
+    )
 
     def add_block(block):
-        lines = kv[block]
-        scores = lax.dot_general(queries[...], lines, contract, preferred_element_type=f32)
+        scores = jnp.dot(queries[...], kv[block, width:], preferred_element_type=f32)
         scores = scores * scores
         weights = jnp.concatenate(
             [scores[:tok] * scale_carried[block], scores[tok:] * scale_final[block]], axis=0
         ).astype(bf16)
-        carried[...] += jnp.dot(weights, lines, preferred_element_type=f32)
+        carried[...] += lax.dot_general(
+            weights, kv[block, :width], contract, preferred_element_type=f32
+        )
 
     forwards = []
     wait_block(peer_x)
@@ -375,27 +376,26 @@
         wait_block(block)
         add_block(block)
 
-    reach_out[...] = carried[tok + cont_pad :]
+    reach_out[:, :width] = carried[tok + cont_pad :]
     reach_copy = send(
         reach_out, reach_in, pair_send.at[1], pair_recv.at[1], {"narrow": sibling}
     )
     reach_copy.start()
 
-    def rms(rows):
-        rows = rows[:, :width]
-        square = jnp.sum(rows * rows, axis=1, keepdims=True) * (1.0 / width)
+    def rms(rows, axis):
+        square = jnp.sum(rows * rows, axis=axis, keepdims=True) * (1.0 / width)
         return rows * lax.rsqrt(square + epsilon)
 
-    result = rms(local + jnp.exp(total_col) * carried[:tok])
-    out_ref[0] = jnp.where(live_col, result, 0.0).astype(bf16)
-
-    row_id = lax.broadcasted_iota(jnp.int32, (cont_pad, 2 * width), 0)
-    prompts = jnp.zeros((cont_pad, 2 * width), jnp.int32)
+    result = rms(jnp.transpose(local + jnp.exp(total_col) * carried[:tok]), 0)
+    out_ref[0] = jnp.where(live_row, result, 0.0).astype(bf16)
+
+    row_id = lax.broadcasted_iota(jnp.int32, (cont_pad, width), 0)
+    prompts = jnp.zeros((cont_pad, width), jnp.int32)
     for r in range(cont_count):
         prompts = jnp.where(row_id == r, prompt_ref[r], prompts)
     reach_copy.wait()
-    reach = jnp.where(prompts == lane, carried[tok : tok + cont_pad], reach_in[...])
-    cont_out_ref[...] = rms(reach)[:cont_count].astype(bf16)
+    reach = jnp.where(prompts == lane, carried[tok : tok + cont_pad], reach_in[:, :width])
+    cont_out_ref[...] = rms(reach, 1)[:cont_count].astype(bf16)
 
     for copy in gate_copies + kv_copies + forwards:
         copy.wait_send()
@@ -403,6 +403,7 @@
 
 def gathered(n, queries, key_rows, values, log_gate, lengths, cont_queries, cont_prompt):
     tok, width = queries.shape[1], queries.shape[2]
+    flat = lambda rows: jnp.transpose(rows, (0, 2, 1))
     cont_count = cont_queries.shape[0]
     cont_pad = -(-cont_count // 16) * 16
     levels = n // 2
@@ -410,24 +411,24 @@
     smem = pl.BlockSpec(memory_space=pltpu.SMEM)
     dma = lambda count: pltpu.SemaphoreType.DMA((count,))
     f32, bf16 = jnp.float32, jnp.bfloat16
-    return pl.pallas_call(
+    prompt_out, cont_out = pl.pallas_call(
         functools.partial(gather_kernel, n),
         name="retention",
         out_shape=(
-            jax.ShapeDtypeStruct((1, tok, width), bf16),
+            jax.ShapeDtypeStruct((1, width, tok), bf16),
             jax.ShapeDtypeStruct((cont_count, width), bf16),
         ),
         in_specs=[smem, smem, vmem, vmem, vmem, vmem, vmem],
         out_specs=(vmem, vmem),
         scratch_shapes=[
-            pltpu.VMEM((n, tok, 2 * width), bf16),
+            pltpu.VMEM((n, 2 * width, tok), bf16),
             pltpu.VMEM((n, 1, tok), f32),
-            pltpu.VMEM((tok + 2 * cont_pad, 2 * width), bf16),
+            pltpu.VMEM((tok + 2 * cont_pad, width), bf16),
             pltpu.VMEM((cont_pad, 2 * width), bf16),
             pltpu.VMEM((cont_pad, 2 * width), bf16),
             pltpu.VMEM((n, 1, tok), f32),
             pltpu.VMEM((n, 1, tok), f32),
-            pltpu.VMEM((tok + 2 * cont_pad, 2 * width), f32),
+            pltpu.VMEM((tok + 2 * cont_pad, width), f32),
             pltpu.VMEM((cont_pad, 2 * width), f32),
             pltpu.VMEM((cont_pad, 2 * width), f32),
             dma(n),
@@ -439,7 +440,8 @@
             dma(2),
         ],
         compiler_params=pltpu.CompilerParams(collective_id=0, has_side_effects=True),
-    )(lengths, cont_prompt, queries, key_rows, values, log_gate, cont_queries)
+    )(lengths, cont_prompt, flat(queries), flat(key_rows), flat(values), log_gate, cont_queries)
+    return flat(prompt_out), cont_out
 
 
 def solution(mesh):

time: 25.6 us -> 22.4 us (0.87)
  local copies, waits for them, and re-layouts: 5.09 us -> 1.96 us
    unnamed x10 -> x4, local copies, waits for them, and re-layouts: 3.55 us -> 1.96 us
    pallas_call x1 -> x0, local copies, waits for them, and re-layouts: 1.54 us -> none  [gathered(): pl.pallas_call(functools.partial(gather_kernel, n), name='retention', out...]
where the time goes in v2:
time: 22.4 us; the launch traced here: 22.1 us
  Pallas kernels  18.9 us (84%)
  local copies, waits for them, and re-layouts  1.96 us (9%)
  between operations  1.29 us (6%)
    pallas_call x1, Pallas kernels, gathered(): pl.pallas_call(functools.partial(gather_kernel, n), name='retention', out...  18.9 us
    unnamed x4, local copies, waits for them, and re-layouts  1.96 us

profile of v2, /device:TPU:0, one launch (start us, length us, event | category | flops | bytes accessed | tf_op | source)
XLA Modules:
  0.0 22.1 jit_solution(11358851400880303324)
XLA Ops:
  1.3 18.9 %retention.1 = (bf16[1,64,256]{2,1,0:T(8,128)(2,1)}, bf16[5,64]{1,0:T(8,128)(2,1)}) custom-call(s32[1]{0:T(128)S(6)} %copy.11.lengths_ref, s32[5]{0:T(128)} %prompt_ref.1, bf16[1,64,256]{2,1,0:T(8,128)(2,1)} %bitcast.4, bf16[1,64,256]{2,1,0:T(8,128)(2,1)} %bitcast.5, bf16[1,64,256]{2,1,0:T(8,128)(2,1)} %bitcast.6, f32[1,256]{1,0:T(1,128)} %gate_ref.1, ...), custom_call_target="tpu_custom_call" | custom-call | tf_op jit(solution)/shard_map/retention/pallas_call | solution.py:414
  20.1 0.0 copy-start
  20.2 1.4 %copy.12 = bf16[1,256,64]{1,2,0:T(8,128)(2,1)} copy(bf16[1,256,64]{1,2,0:T(8,128)(2,1)} %bitcast.7) | data formatting | bytes 65536
  21.5 0.0 copy-done
  21.5 0.6 %copy.13 = bf16[5,64]{1,0:T(8,128)(2,1)} copy(bf16[5,64]{1,0:T(8,128)(2,1)S(1)} %copy-done) | data formatting | bytes 1280
Async XLA Ops:
  20.1 1.4 %copy-start = (bf16[5,64]{1,0:T(8,128)(2,1)S(1)}, bf16[5,64]{1,0:T(8,128)(2,1)}, u32[]{:S(2)}) copy-start(bf16[5,64]{1,0:T(8,128)(2,1)} %get-tuple-element.9) | copy-start | bytes 1924

commit v3 on v2

--- a/solution.py
+++ b/solution.py
@@ -205,13 +205,15 @@
     n,
     lengths_ref,
     prompt_ref,
-    query_ref,
-    key_ref,
-    value_ref,
+    query_hbm,
+    key_hbm,
+    value_hbm,
     gate_ref,
     cont_ref,
     out_ref,
     cont_out_ref,
+    query_ref,
+    load_sem,
     kv,
     gates,
     queries,
@@ -235,7 +237,7 @@
     lane = lax.axis_index("narrow")
     row, side = me // 2, me % 2
     levels = n // 2
-    width, tok = query_ref.shape[1], query_ref.shape[2]
+    width, tok = query_ref.shape
     cont_count = cont_ref.shape[0]
     cont_pad = cont_own.shape[0]
     mesh_id = pl.DeviceIdType.MESH
@@ -250,9 +252,14 @@
         )
     pl.semaphore_signal(barrier, inc=1, device_id={"narrow": sibling}, device_id_type=mesh_id)
 
-    kv[me] = jnp.concatenate([value_ref[0], key_ref[0]], axis=0)
+    loads = [
+        pltpu.make_async_copy(value_hbm.at[0], kv.at[me, :width], load_sem.at[0]),
+        pltpu.make_async_copy(key_hbm.at[0], kv.at[me, width:], load_sem.at[1]),
+        pltpu.make_async_copy(query_hbm.at[0], query_ref, load_sem.at[2]),
+    ]
+    for load in loads:
+        load.start()
     gates[me] = gate_ref[...]
-    queries[:tok] = jnp.transpose(query_ref[0])
     cont_own[...] = jnp.zeros_like(cont_own)
     cont_own[:cont_count, :width] = cont_ref[...]
 
@@ -266,6 +273,9 @@
             device_id_type=mesh_id,
         )
 
+    for load in loads:
+        load.wait()
+    queries[:tok] = jnp.transpose(query_ref[...])
     pl.semaphore_wait(barrier, n)
 
     gate_copies = []
@@ -274,13 +284,27 @@
         gate_copies.append(
             send(gate_ref, gates.at[me], gate_send.at[step], gate_recv.at[step], {"wide": to})
         )
+    def x_move(block, half, bits):
+        lines = kv.at[block, pl.ds(half * width, width)]
+        return send(
+            lines, lines, x_send.at[bits, half], kv_recv.at[block, half], {"wide": peer_x}
+        )
+
     kv_copies = []
     for bits in tuple(reversed(sorted(order))):
         to = 2 * flip(row, bits) + side
-        kv_copies.append(
-            send(kv.at[me], kv.at[me], col_send.at[bits], kv_recv.at[me], {"wide": to})
-        )
-    kv_copies.append(send(kv.at[me], kv.at[me], x_send.at[0], kv_recv.at[me], {"wide": peer_x}))
+        for half in range(2):
+            kv_copies.append(
+                send(
+                    kv.at[me, pl.ds(half * width, width)],
+                    kv.at[me, pl.ds(half * width, width)],
+                    col_send.at[bits, half],
+                    kv_recv.at[me, half],
+                    {"wide": to},
+                )
+            )
+    for half in range(2):
+        kv_copies.append(x_move(me, half, 0))
     cont_copy = send(
         cont_own, cont_other, pair_send.at[0], pair_recv.at[0], {"narrow": sibling}
     )
@@ -291,14 +315,12 @@
     cont_copy.start()
 
     def wait_block(block):
-        send(
-            kv.at[block], kv.at[block], x_send.at[0], kv_recv.at[block], {"wide": peer_x}
-        ).wait_recv()
-
-    def forward(block, bits):
-        copy = send(
-            kv.at[block], kv.at[block], x_send.at[bits], kv_recv.at[block], {"wide": peer_x}
-        )
+        for half in range(2):
+            x_move(block, half, 0).wait_recv()
+
+    def forward(block, bits, half):
+        copy = x_move(block, half, bits)
+        copy.wait_recv()
         copy.start()
         return copy
 
@@ -313,10 +335,10 @@
     total_col = jnp.sum(jnp.where(lower, gate_row, 0.0), axis=1, keepdims=True)
     total_row = prefix_sums(jnp.broadcast_to(gate_row, (8, tok)), upper)[:1]
     contract = (((1,), (1,)), ((), ()))
-    scores = jnp.dot(queries[:tok], key_ref[0], preferred_element_type=f32)
+    scores = jnp.dot(queries[:tok], kv[me, width:], preferred_element_type=f32)
     decay = jnp.exp(jnp.where(lower & live_row, total_col - total_row, -jnp.inf))
     local = lax.dot_general(
-        (scores * scores * decay).astype(bf16), value_ref[0], contract, preferred_element_type=f32
+        (scores * scores * decay).astype(bf16), kv[me, :width], contract, preferred_element_type=f32
     )
 
     for step in range(1, n):
@@ -346,11 +368,11 @@
     queries[tok : tok + cont_pad] = cont_own[:, :width]
     queries[tok + cont_pad :] = cont_other[:, :width]
 
-    cont_scores = jnp.dot(queries[tok:], key_ref[0], preferred_element_type=f32)
+    cont_scores = jnp.dot(queries[tok:], kv[me, width:], preferred_element_type=f32)
     cont_weights = (cont_scores * cont_scores * scale_final[me]).astype(bf16)
     carried[:tok] = jnp.zeros((tok, width), f32)
     carried[tok:] = lax.dot_general(
-        cont_weights, value_ref[0], contract, preferred_element_type=f32
+        cont_weights, kv[me, :width], contract, preferred_element_type=f32
     )
 
     def add_block(block):
@@ -364,13 +386,13 @@
         )
 
     forwards = []
+    for bits in order:
+        block = 2 * flip(row, bits) + side
+        for half in range(2):
+            forwards.append(forward(block, bits, half))
+        add_block(block)
     wait_block(peer_x)
     add_block(peer_x)
-    for bits in order:
-        block = 2 * flip(row, bits) + side
-        wait_block(block)
-        forwards.append(forward(block, bits))
-        add_block(block)
     for bits in order:
         block = 2 * flip(row, bits) + 1 - side
         wait_block(block)
@@ -401,6 +423,11 @@
         copy.wait_send()
 
 
+def finish_kernel(prompt_ref, cont_ref, prompt_out_ref, cont_out_ref):
+    prompt_out_ref[...] = prompt_ref[...]
+    cont_out_ref[...] = cont_ref[...]
+
+
 def gathered(n, queries, key_rows, values, log_gate, lengths, cont_queries, cont_prompt):
     tok, width = queries.shape[1], queries.shape[2]
     flat = lambda rows: jnp.transpose(rows, (0, 2, 1))
@@ -408,6 +435,7 @@
     cont_pad = -(-cont_count // 16) * 16
     levels = n // 2
     vmem = pl.BlockSpec(memory_space=pltpu.VMEM)
+    hbm = pl.BlockSpec(memory_space=pl.ANY)
     smem = pl.BlockSpec(memory_space=pltpu.SMEM)
     dma = lambda count: pltpu.SemaphoreType.DMA((count,))
     f32, bf16 = jnp.float32, jnp.bfloat16
@@ -418,9 +446,11 @@
             jax.ShapeDtypeStruct((1, width, tok), bf16),
             jax.ShapeDtypeStruct((cont_count, width), bf16),
         ),
-        in_specs=[smem, smem, vmem, vmem, vmem, vmem, vmem],
+        in_specs=[smem, smem, hbm, hbm, hbm, vmem, vmem],
         out_specs=(vmem, vmem),
         scratch_shapes=[
+            pltpu.VMEM((width, tok), bf16),
+            dma(3),
             pltpu.VMEM((n, 2 * width, tok), bf16),
             pltpu.VMEM((n, 1, tok), f32),
             pltpu.VMEM((tok + 2 * cont_pad, width), bf16),
@@ -433,14 +463,24 @@
             pltpu.VMEM((cont_pad, 2 * width), f32),
             dma(n),
             dma(n),
-            dma(levels),
-            dma(levels),
-            dma(n),
+            pltpu.SemaphoreType.DMA((levels, 2)),
+            pltpu.SemaphoreType.DMA((levels, 2)),
+            pltpu.SemaphoreType.DMA((n, 2)),
             dma(2),
             dma(2),
         ],
         compiler_params=pltpu.CompilerParams(collective_id=0, has_side_effects=True),
     )(lengths, cont_prompt, flat(queries), flat(key_rows), flat(values), log_gate, cont_queries)
+    prompt_out, cont_out = pl.pallas_call(
+        finish_kernel,
+        name="finish",
+        out_shape=(
+            jax.ShapeDtypeStruct(prompt_out.shape, bf16),
+            jax.ShapeDtypeStruct(cont_out.shape, bf16),
+        ),
+        in_specs=[vmem, vmem],
+        out_specs=(vmem, vmem),
+    )(prompt_out, cont_out)
     return flat(prompt_out), cont_out
 
 

time: 22.4 us -> 21.6 us (0.964)
  local copies, waits for them, and re-layouts: 1.96 us -> 0 us
  Pallas kernels: 18.9 us -> 20 us
    unnamed x4 -> x0, local copies, waits for them, and re-layouts: 1.96 us -> none
    pallas_call x0 -> x1, Pallas kernels: none -> 1.38 us  [gathered(): pl.pallas_call(finish_kernel, name='finish', out_shape=(jax.ShapeDtypeStr...]
    pallas_call x1, Pallas kernels: 18.9 us -> 18.6 us  [gathered(): pl.pallas_call(functools.partial(gather_kernel, n), name='retention', out...]
where the time goes in v3:
time: 21.6 us; the launch traced here: 21.3 us
  Pallas kernels  20 us (93%)
  between operations  1.29 us (6%)
    pallas_call x1, Pallas kernels, gathered(): pl.pallas_call(functools.partial(gather_kernel, n), name='retention', out...  18.6 us
    pallas_call x1, Pallas kernels, gathered(): pl.pallas_call(finish_kernel, name='finish', out_shape=(jax.ShapeDtypeStr...  1.38 us

profile of v3, /device:TPU:0, one launch (start us, length us, event | category | flops | bytes accessed | tf_op | source)
XLA Modules:
  0.0 21.3 jit_solution(15675532963623649901)
XLA Ops:
  1.3 18.6 %retention.1 = (bf16[1,64,256]{2,1,0:T(8,128)(2,1)}, bf16[5,64]{1,0:T(8,128)(2,1)}) custom-call(s32[1]{0:T(128)S(6)} %copy.9.lengths_ref, s32[5]{0:T(128)} %prompt_ref.1, bf16[1,64,256]{2,1,0:T(8,128)(2,1)} %bitcast.4, bf16[1,64,256]{2,1,0:T(8,128)(2,1)} %bitcast.5, bf16[1,64,256]{2,1,0:T(8,128)(2,1)} %bitcast.6, f32[1,256]{1,0:T(1,128)} %gate_ref.1, ...), custom_call_target="tpu_custom_call" | custom-call | tf_op jit(solution)/shard_map/retention/pallas_call | solution.py:442
  19.9 1.4 %finish.1 = (bf16[1,64,256]{2,1,0:T(8,128)(2,1)}, bf16[5,64]{1,0:T(8,128)(2,1)}) custom-call(bf16[1,64,256]{2,1,0:T(8,128)(2,1)} %get-tuple-element.6.prompt_ref, bf16[5,64]{1,0:T(8,128)(2,1)} %get-tuple-element.7.cont_ref), custom_call_target="tpu_custom_call" | custom-call | tf_op jit(solution)/shard_map/finish/pallas_call | solution.py:474
